TPU v7x, 256 devices: a whole 4x4x8 slice. The times are simulated.
256 devices in a mesh: dp: 8 (over z), seq: 32 (over x, y, core).
Axes of the slice: x: 4, y: 4, z: 8, core: 2. Of those that a mesh axis runs over, the one named last changes fastest.
Arguments:
- seq_in: bfloat16 [65536, 1536], P(('dp', 'seq')), parts along dimension 0, may hold values from -6 to 6
- conv_gain: float32 [1536], replicated, may hold values from 0.1 to 1.9
- convolution_weight: bfloat16 [3, 1536, 768], replicated, may hold values from -0.09375 to 0.09375
- conv_bias: float32 [768], replicated, may hold values from -3 to 3
- attn_gain: float32 [1536], replicated, may hold values from 0.1 to 1.9
- w_query: bfloat16 [1536, 512], replicated
- w_key: bfloat16 [1536, 128], replicated
- w_value: bfloat16 [1536, 128], replicated, may hold values from -0.15625 to 0.15625
- w_out: bfloat16 [512, 1536], replicated, may hold values from -0.25 to 0.25
Outputs:
- block_out: bfloat16 [65536, 1536], P(('dp', 'seq')), parts along dimension 0
There are 8 independent parts, one for each index of `dp`. A program takes and returns all parts, laid end to end along the dimension named above; an argument that names none is the same for every part. Nothing has to cross between parts.
All inputs are finite; a program needn't handle non-finite values.
Results may differ from a plain program's by a relative error of at most 0.0059.
Values may be sent and summed in bfloat16 or wider, within the bound.
A program may use at most 128 MiB of HBM per device.

v0:
```python
import jax
import jax.numpy as jnp
from jax import lax
from jax.sharding import PartitionSpec as P

DILATION_STEP = 4


def padded(cells, sides, width):
    for axis, dim in sides:
        count = lax.axis_size(axis)
        ends = count - 1
        head = lax.slice_in_dim(cells, 0, width, axis=dim)
        tail = lax.slice_in_dim(cells, cells.shape[dim] - width, cells.shape[dim], axis=dim)
        cells = jnp.concatenate(
            [
                lax.ppermute(tail, axis, [(i, (i + 1) % count) for i in range(ends)]),
                cells,
                lax.ppermute(head, axis, [((i + 1) % count, i) for i in range(ends)]),
            ],
            axis=dim,
        )
    return cells


def normalize(values, gain_vec):
    wide = values.astype(jnp.float32)
    meansq = jnp.mean(wide * wide, axis=-1, keepdims=True)
    return wide * lax.rsqrt(meansq + 1e-06) * gain_vec


def fold_block(state_now, keys_vals, queries, head_dim):
    maxima, totals, summed = state_now
    key_part = keys_vals[:, :head_dim]
    value_part = keys_vals[:, head_dim:]
    scores = jnp.einsum(
        "thd,kd->htk", queries, key_part, preferred_element_type=jnp.float32
    ) * head_dim ** (-0.5)
    new_max = jnp.maximum(maxima, jnp.max(scores, axis=-1))
    factor = jnp.exp(maxima - new_max)
    expd = jnp.exp(scores - new_max[..., None])
    totals = totals * factor + jnp.sum(expd, axis=-1)
    summed = summed * factor[..., None] + jnp.einsum(
        "htk,kd->htd", expd.astype(jnp.bfloat16), value_part, preferred_element_type=jnp.float32
    )
    return (new_max, totals, summed)


def body(
    seq_in, conv_gain, convolution_weight, conv_bias, attn_gain, w_query, w_key, w_value, w_out
):
    token_rows = seq_in.shape[0]
    kernel_taps = convolution_weight.shape[0]
    head_dim = w_key.shape[1]
    heads_all = w_query.shape[1] // head_dim
    out_chan = convolution_weight.shape[2]
    receptive_reach = DILATION_STEP * (kernel_taps - 1) // 2
    normed = normalize(seq_in, conv_gain).astype(jnp.bfloat16)
    padded_tokens = padded(normed, (("seq", 0),), receptive_reach)
    convolved_total = jnp.dot(
        padded_tokens[0:token_rows], convolution_weight[0], preferred_element_type=jnp.float32
    )
    for tap_index in range(1, kernel_taps):
        convolved_total = convolved_total + jnp.dot(
            padded_tokens[tap_index * DILATION_STEP : tap_index * DILATION_STEP + token_rows],
            convolution_weight[tap_index],
            preferred_element_type=jnp.float32,
        )
    activated = jax.nn.gelu(convolved_total + conv_bias, approximate=True)
    wide_in = seq_in.astype(jnp.float32)
    hidden = jnp.concatenate(
        [wide_in[:, :out_chan] + activated, wide_in[:, out_chan:]], axis=1
    ).astype(jnp.bfloat16)
    attn_in = normalize(hidden, attn_gain).astype(jnp.bfloat16)
    queries = jnp.dot(attn_in, w_query, preferred_element_type=jnp.float32).astype(jnp.bfloat16)
    queries = queries.reshape(token_rows, heads_all, head_dim)
    key_rows = jnp.dot(attn_in, w_key, preferred_element_type=jnp.float32).astype(jnp.bfloat16)
    value_rows = jnp.dot(attn_in, w_value, preferred_element_type=jnp.float32).astype(jnp.bfloat16)
    packed = jnp.concatenate([key_rows, value_rows], axis=1)
    start_state = (
        jnp.full((heads_all, token_rows), -1e30, jnp.float32),
        jnp.zeros((heads_all, token_rows), jnp.float32),
        jnp.zeros((heads_all, token_rows, head_dim), jnp.float32),
    )
    gathered = lax.all_gather(packed, "seq", axis=0, tiled=True)
    shards = lax.axis_size("seq")
    group = 1
    for g in range(1, shards + 1):
        if shards % g == 0 and g * token_rows <= 2048:
            group = g
    span = token_rows * group
    count = gathered.shape[0] // span

    def step_keys(block_index, state_now):
        block_rows = lax.dynamic_slice_in_dim(gathered, block_index * span, span, 0)
        return fold_block(state_now, block_rows, queries, head_dim)

    final_state = lax.fori_loop(0, count, step_keys, start_state)
    maxima, totals, summed = final_state
    result = summed / totals[..., None]
    attended = (
        jnp.transpose(result, (1, 0, 2))
        .reshape(token_rows, heads_all * head_dim)
        .astype(jnp.bfloat16)
    )
    mixed = hidden.astype(jnp.float32) + jnp.dot(
        attended, w_out, preferred_element_type=jnp.float32
    )
    return mixed.astype(jnp.bfloat16)


def solution(mesh):
    placed = (P(("dp", "seq"), None), P(), P(), P(), P(), P(), P(), P(), P())
    return jax.shard_map(
        body, mesh=mesh, in_specs=placed, out_specs=P(("dp", "seq"), None), check_vma=False
    )
```

profile of v0, /device:TPU:1, one launch (start us, length us, event | category | flops | bytes accessed | tf_op | source)
XLA Modules:
  0.0 116.0 jit_solution(7414915342071189569)
XLA Ops:
  6.5 0.0 copy-start
  6.5 0.0 all-gather.2.cloned.1.call-start
  6.5 1.5 %multiply_reduce_fusion = f32[256]{0:T(256)S(1)} fusion(bf16[256,1536]{1,0:T(8,128)(2,1)} %param.11), kind=kLoop, calls=%fused_computation.34 | loop fusion | flops 1179392 | bytes 787456 | tf_op jit(solution)/shard_map/reduce_sum | solution.py:28
  8.0 1.4 %multiply_convert_fusion = bf16[256,1536]{1,0:T(8,128)(2,1)S(1)} fusion(f32[1536]{0:T(1024)} %param.12, f32[256]{0:T(256)S(1)} %add_rsqrt_fusion.1, bf16[256,1536]{1,0:T(8,128)(2,1)} %param.11), kind=kLoop, calls=%fused_computation.33 | loop fusion | flops 1572864 | bytes 1580032 | tf_op jit(solution)/shard_map/convert_element_type | solution.py:58
  9.5 4.6 %collective-permute-start = (bf16[4,1536]{1,0:T(4,128)(2,1)S(1)}, bf16[4,1536]{1,0:T(4,128)(2,1)S(1)}, u32[]{:S(2)}, u32[]{:S(2)}) collective-permute-start(bf16[4,1536]{1,0:T(4,128)(2,1)S(1)} %get-tuple-element.166), channel_id=1, source_target_pairs={{0,1},{1,2},{2,3},{3,4},{4,5},{5,6},{6,7},{7,8},{8,9},{9,10},{10,1... | collective-permute-start | bytes 36872 | tf_op jit(solution)/shard_map/ppermute | solution.py:17
  14.1 0.0 copy-start.1
  14.1 2.1 %collective-permute-start.1 = (bf16[4,1536]{1,0:T(4,128)(2,1)S(1)}, bf16[4,1536]{1,0:T(4,128)(2,1)S(1)}, u32[]{:S(2)}, u32[]{:S(2)}) collective-permute-start(bf16[4,1536]{1,0:T(4,128)(2,1)S(1)} %get-tuple-element.167), channel_id=1, source_target_pairs={{1,0},{2,1},{3,2},{4,3},{5,4},{6,5},{7,6},{8,7},{9,8},{10,9},{11,1... | collective-permute-start | bytes 36872 | tf_op jit(solution)/shard_map/ppermute | solution.py:19
  16.1 0.0 copy-start.2
  16.1 2.6 %fusion.15 = f32[256,768]{1,0:T(8,128)S(1)} fusion(bf16[256,1536]{1,0:T(8,128)(2,1)S(1)} %multiply_convert_fusion, bf16[3,1536,768]{2,1,0:T(8,128)(2,1)} %param.13), kind=kOutput, calls=%fused_computation.23 | convolution fusion | flops 603979776 | bytes 3932160 | tf_op jit(solution)/shard_map/dot_general | solution.py:64
  18.7 0.0 copy-done.1
  18.8 0.2 convert_element_type.43
  19.0 0.0 copy-start.6
  19.0 0.2 collective-permute-done.1
  19.2 0.6 copy-done.2
  19.8 0.8 fusion.13
  20.6 0.0 copy-start.3
  20.7 0.0 copy-start.5
  20.7 0.0 collective-permute-done
  20.7 0.0 copy-done.6
  20.7 1.0 fusion.47
  21.7 0.0 copy-start.4
  21.7 0.2 fusion.22
  22.0 0.0 copy-done.3
  22.0 0.0 copy-done.5
  22.0 0.5 convolution_convert_fusion.1
  22.5 0.2 copy-done.4
  22.7 0.5 convolution_convert_fusion.2
  23.2 0.7 pad_maximum_fusion.5
  23.9 0.0 all-gather.2.cloned.1.call-update
  23.9 2.0 %fusion.34 = bf16[32,4,8,128]{3,2,1,0:T(8,128)(2,1)S(1)} fusion(bf16[1536,512]{1,0:T(8,128)(2,1)} %param.16, f32[1536]{0:T(1024)S(1)} %copy-done.5, f32[256]{0:T(256)S(1)} %add_rsqrt_fusion, bf16[256,768]{1,0:T(8,128)(2,1)S(1)} %slice.52, bf16[256,768]{1,0:T(8,128)(2,1)S(1)} %fusion.47), kind=kOutput, calls=%fused_computation.40 | convolution fusion | flops 405536768 | bytes 2628608 | tf_op jit(solution)/shard_map/dot_general | solution.py:75
  26.0 55.1 %all-gather.2.cloned.1.call-done = bf16[8192,256]{0,1:T(8,128)(2,1)} async-done(((bf16[256,256]{0,1:T(8,128)(2,1)}), bf16[8192,256]{0,1:T(8,128)(2,1)}) %all-gather.2.cloned.1.call-update) | async-done | bytes 4194320 | tf_op jit(solution)/shard_map/all_gather | solution.py:85
  81.1 26.3 %while.18 = (s32[]{:T(128)}, f32[4,256]{1,0:T(4,128)S(1)}, f32[4,256]{1,0:T(4,128)S(1)}, f32[4,256,128]{2,1,0:T(8,128)S(1)}, bf16[8192,256]{0,1:T(8,128)(2,1)}, ...) while((s32[]{:T(128)}, f32[4,256]{1,0:T(4,128)S(1)}, ...), condition=%wide.region_5.0_spmd.clone, body=%wide.region_2.0_spmd.clone.sunk | while | flops 1090917376 | bytes 27590852 | solution.py:98
  81.1 2.3 %bitcast_reduce_fusion.2 = (f32[4,256]{1,0:T(4,128)S(1)}, f32[2048,256,4]{1,0,2:T(8,128)S(1)}) fusion(bf16[256,4,128]{2,0,1:T(8,128)(2,1)S(1)} %get-tuple-element.240, bf16[8192,256]{0,1:T(8,128)(2,1)} %get-tuple-element.239, s32[]{:T(128)S(6)} %select_n.9), kind=kOutput, calls=%fused_computation.1.clone.1 | convolution fusion | flops 541064192 | bytes 9179140 | tf_op jit(solution)/shard_map/while/body/eval_jaxpr/thd,kd->htk/dot_general | solution.py:36
  83.4 1.4 %fusion.72 = f32[4,256]{1,0:T(4,128)S(1)} fusion(f32[2048,256,4]{1,0,2:T(8,128)S(1)} %get-tuple-element.210, f32[4,256]{1,0:T(4,128)S(1)} %select_maximum_fusion.2), kind=kLoop, calls=%fused_computation.4.clone.1 | loop fusion | flops 6290432 | bytes 8396800 | tf_op jit(solution)/shard_map/while/body/eval_jaxpr/reduce_sum | solution.py:42
  84.8 2.8 %fusion.74 = f32[4,256,128]{2,1,0:T(8,128)S(1)} fusion(f32[2048,256,4]{1,0,2:T(8,128)S(1)} %get-tuple-element.210, f32[4,256]{1,0:T(4,128)S(1)} %select_maximum_fusion.2, bf16[8192,256]{0,1:T(8,128)(2,1)} %get-tuple-element.239, s32[]{:T(128)S(6)} %select_n.9, s32[]{:T(128)S(6)} %add.170, f32[4,256,128]{2,1,0:T(8,128)S(1)} %get-tuple-element.227, ...), kind=kOutput, calls=%fused_computation.6.clone.1 | convolution fusion | flops 543555584 | bytes 9969673 | tf_op jit(solution)/shard_map/while/body/eval_jaxpr/htk,kd->htd/dot_general | solution.py:43
  87.7 2.4 %bitcast_reduce_fusion.2 = (f32[4,256]{1,0:T(4,128)S(1)}, f32[2048,256,4]{1,0,2:T(8,128)S(1)}) fusion(bf16[256,4,128]{2,0,1:T(8,128)(2,1)S(1)} %get-tuple-element.240, bf16[8192,256]{0,1:T(8,128)(2,1)} %get-tuple-element.239, s32[]{:T(128)S(6)} %select_n.9), kind=kOutput, calls=%fused_computation.1.clone.1 | convolution fusion | flops 541064192 | bytes 9179140 | tf_op jit(solution)/shard_map/while/body/eval_jaxpr/thd,kd->htk/dot_general | solution.py:36
  90.0 1.4 %fusion.72 = f32[4,256]{1,0:T(4,128)S(1)} fusion(f32[2048,256,4]{1,0,2:T(8,128)S(1)} %get-tuple-element.210, f32[4,256]{1,0:T(4,128)S(1)} %select_maximum_fusion.2), kind=kLoop, calls=%fused_computation.4.clone.1 | loop fusion | flops 6290432 | bytes 8396800 | tf_op jit(solution)/shard_map/while/body/eval_jaxpr/reduce_sum | solution.py:42
  91.4 2.8 %fusion.74 = f32[4,256,128]{2,1,0:T(8,128)S(1)} fusion(f32[2048,256,4]{1,0,2:T(8,128)S(1)} %get-tuple-element.210, f32[4,256]{1,0:T(4,128)S(1)} %select_maximum_fusion.2, bf16[8192,256]{0,1:T(8,128)(2,1)} %get-tuple-element.239, s32[]{:T(128)S(6)} %select_n.9, s32[]{:T(128)S(6)} %add.170, f32[4,256,128]{2,1,0:T(8,128)S(1)} %get-tuple-element.227, ...), kind=kOutput, calls=%fused_computation.6.clone.1 | convolution fusion | flops 543555584 | bytes 9969673 | tf_op jit(solution)/shard_map/while/body/eval_jaxpr/htk,kd->htd/dot_general | solution.py:43
  94.3 2.4 %bitcast_reduce_fusion.2 = (f32[4,256]{1,0:T(4,128)S(1)}, f32[2048,256,4]{1,0,2:T(8,128)S(1)}) fusion(bf16[256,4,128]{2,0,1:T(8,128)(2,1)S(1)} %get-tuple-element.240, bf16[8192,256]{0,1:T(8,128)(2,1)} %get-tuple-element.239, s32[]{:T(128)S(6)} %select_n.9), kind=kOutput, calls=%fused_computation.1.clone.1 | convolution fusion | flops 541064192 | bytes 9179140 | tf_op jit(solution)/shard_map/while/body/eval_jaxpr/thd,kd->htk/dot_general | solution.py:36
  96.6 1.4 %fusion.72 = f32[4,256]{1,0:T(4,128)S(1)} fusion(f32[2048,256,4]{1,0,2:T(8,128)S(1)} %get-tuple-element.210, f32[4,256]{1,0:T(4,128)S(1)} %select_maximum_fusion.2), kind=kLoop, calls=%fused_computation.4.clone.1 | loop fusion | flops 6290432 | bytes 8396800 | tf_op jit(solution)/shard_map/while/body/eval_jaxpr/reduce_sum | solution.py:42
  98.0 2.8 %fusion.74 = f32[4,256,128]{2,1,0:T(8,128)S(1)} fusion(f32[2048,256,4]{1,0,2:T(8,128)S(1)} %get-tuple-element.210, f32[4,256]{1,0:T(4,128)S(1)} %select_maximum_fusion.2, bf16[8192,256]{0,1:T(8,128)(2,1)} %get-tuple-element.239, s32[]{:T(128)S(6)} %select_n.9, s32[]{:T(128)S(6)} %add.170, f32[4,256,128]{2,1,0:T(8,128)S(1)} %get-tuple-element.227, ...), kind=kOutput, calls=%fused_computation.6.clone.1 | convolution fusion | flops 543555584 | bytes 9969673 | tf_op jit(solution)/shard_map/while/body/eval_jaxpr/htk,kd->htd/dot_general | solution.py:43
  100.8 2.4 %bitcast_reduce_fusion.2 = (f32[4,256]{1,0:T(4,128)S(1)}, f32[2048,256,4]{1,0,2:T(8,128)S(1)}) fusion(bf16[256,4,128]{2,0,1:T(8,128)(2,1)S(1)} %get-tuple-element.240, bf16[8192,256]{0,1:T(8,128)(2,1)} %get-tuple-element.239, s32[]{:T(128)S(6)} %select_n.9), kind=kOutput, calls=%fused_computation.1.clone.1 | convolution fusion | flops 541064192 | bytes 9179140 | tf_op jit(solution)/shard_map/while/body/eval_jaxpr/thd,kd->htk/dot_general | solution.py:36
  103.2 1.4 %fusion.72 = f32[4,256]{1,0:T(4,128)S(1)} fusion(f32[2048,256,4]{1,0,2:T(8,128)S(1)} %get-tuple-element.210, f32[4,256]{1,0:T(4,128)S(1)} %select_maximum_fusion.2), kind=kLoop, calls=%fused_computation.4.clone.1 | loop fusion | flops 6290432 | bytes 8396800 | tf_op jit(solution)/shard_map/while/body/eval_jaxpr/reduce_sum | solution.py:42
  104.6 2.8 %fusion.74 = f32[4,256,128]{2,1,0:T(8,128)S(1)} fusion(f32[2048,256,4]{1,0,2:T(8,128)S(1)} %get-tuple-element.210, f32[4,256]{1,0:T(4,128)S(1)} %select_maximum_fusion.2, bf16[8192,256]{0,1:T(8,128)(2,1)} %get-tuple-element.239, s32[]{:T(128)S(6)} %select_n.9, s32[]{:T(128)S(6)} %add.170, f32[4,256,128]{2,1,0:T(8,128)S(1)} %get-tuple-element.227, ...), kind=kOutput, calls=%fused_computation.6.clone.1 | convolution fusion | flops 543555584 | bytes 9969673 | tf_op jit(solution)/shard_map/while/body/eval_jaxpr/htk,kd->htd/dot_general | solution.py:43
  107.4 0.2 copy.16
  107.7 0.0 copy-done
  107.7 1.5 %fusion.12 = bf16[256,1536]{1,0:T(8,128)(2,1)} fusion(bf16[256,512]{0,1:T(8,128)(2,1)S(1)} %bitcast.71, bf16[512,1536]{1,0:T(8,128)(2,1)S(1)} %copy-done, bf16[256,768]{1,0:T(8,128)(2,1)S(1)} %slice.52, bf16[256,768]{1,0:T(8,128)(2,1)S(1)} %fusion.47), kind=kOutput, calls=%fused_computation.18 | convolution fusion | flops 405012480 | bytes 3407872 | tf_op jit(solution)/shard_map/dot_general | solution.py:106
  (21 shorter events, 0.3 us)
Async XLA Ops:
  6.5 101.2 %copy-start = (bf16[512,1536]{1,0:T(8,128)(2,1)S(1)}, bf16[512,1536]{1,0:T(8,128)(2,1)}, u32[]{:S(2)}) copy-start(bf16[512,1536]{1,0:T(8,128)(2,1)} %param.19) | copy-start | bytes 4718596
  6.5 74.5 %all-gather.2.cloned.1.call-start = ((), (), s32[]{:S(2)}) async-start(), calls=%async_computation | async-start | bytes 4325376 | tf_op jit(solution)/shard_map/all_gather | solution.py:85
  9.5 11.2 %collective-permute-start = (bf16[4,1536]{1,0:T(4,128)(2,1)S(1)}, bf16[4,1536]{1,0:T(4,128)(2,1)S(1)}, u32[]{:S(2)}, u32[]{:S(2)}) collective-permute-start(bf16[4,1536]{1,0:T(4,128)(2,1)S(1)} %get-tuple-element.166), channel_id=1, source_target_pairs={{0,1},{1,2},{2,3},{3,4},{4,5},{5,6},{6,7},{7,8},{8,9},{9,10},{10,1... | collective-permute-start | bytes 36872 | tf_op jit(solution)/shard_map/ppermute | solution.py:17
  14.1 4.7 %copy-start.1 = (bf16[256,1536]{1,0:T(8,128)(2,1)S(1)}, bf16[256,1536]{1,0:T(8,128)(2,1)}, u32[]{:S(2)}) copy-start(bf16[256,1536]{1,0:T(8,128)(2,1)} %param.11) | copy-start | bytes 2359300
  14.1 5.1 %collective-permute-start.1 = (bf16[4,1536]{1,0:T(4,128)(2,1)S(1)}, bf16[4,1536]{1,0:T(4,128)(2,1)S(1)}, u32[]{:S(2)}, u32[]{:S(2)}) collective-permute-start(bf16[4,1536]{1,0:T(4,128)(2,1)S(1)} %get-tuple-element.167), channel_id=1, source_target_pairs={{1,0},{2,1},{3,2},{4,3},{5,4},{6,5},{7,6},{8,7},{9,8},{10,9},{11,1... | collective-permute-start | bytes 36872 | tf_op jit(solution)/shard_map/ppermute | solution.py:19
  16.1 3.7 %copy-start.2 = (bf16[3,1536,768]{2,1,0:T(8,128)(2,1)S(1)}, bf16[3,1536,768]{2,1,0:T(8,128)(2,1)}, u32[]{:S(2)}) copy-start(bf16[3,1536,768]{2,1,0:T(8,128)(2,1)} %param.13) | copy-start | bytes 21233668
  19.0 1.7 %copy-start.6 = (f32[768]{0:T(1024)S(1)}, f32[768]{0:T(1024)}, u32[]{:S(2)}) copy-start(f32[768]{0:T(1024)} %param.14) | copy-start | bytes 9220
  20.6 1.3 %copy-start.3 = (bf16[1536,128]{1,0:T(8,128)(2,1)S(1)}, bf16[1536,128]{1,0:T(8,128)(2,1)}, u32[]{:S(2)}) copy-start(bf16[1536,128]{1,0:T(8,128)(2,1)} %param.18) | copy-start | bytes 1179652
  20.7 1.3 %copy-start.5 = (f32[1536]{0:T(1024)S(1)}, f32[1536]{0:T(1024)}, u32[]{:S(2)}) copy-start(f32[1536]{0:T(1024)} %param.15) | copy-start | bytes 18436
  21.7 1.0 copy-start.4
Sparse Core Ops, SparseCore 0:
  24.0 57.0 all-gather.1
where the time goes:
time: 117 us; the launch traced here: 116 us
  waiting for transfers between devices  55.3 us (47%)
  matrix products  29.4 us (25%)
  between operations  13.6 us (12%)
  other arithmetic  9.62 us (8%)
  starting transfers between devices  6.64 us (6%)
  local copies, waits for them, and re-layouts  1.19 us (1%)
    all_gather x1, waiting for transfers between devices, body(): gathered = lax.all_gather(packed, 'seq', axis=0, tiled=True)  55.1 us
    dot_general x4, matrix products, fold_block(): jnp.einsum('htk,kd->htd', expd.astype(jnp.bfloat16), value_part, preferre...  11.2 us
    dot_general x4, matrix products, fold_block(): jnp.einsum('thd,kd->htk', queries, key_part, preferred_element_type=jnp.f...  9.4 us
    reduce_sum x4, other arithmetic, fold_block(): totals = totals * factor + jnp.sum(expd, axis=-1)  5.49 us
    ppermute x1, starting transfers between devices, padded(): lax.ppermute(tail, axis, [(i, (i + 1) % count) for i in range(ends)])  4.58 us
    dot_general x2, matrix products, body(): jnp.dot(padded_tokens[tap_index * DILATION_STEP:tap_index * DILATION_STEP...  3.38 us
  transfers between devices with their start and end apart: 3, of which 2 were waited for; matrix products, arithmetic and copies ran while one was open for 5% of the time, Pallas kernels for 0%

commit v1 on v0

v1 whole, which is shorter than its diff:
```python
import jax
import jax.numpy as jnp
from jax import lax
from jax.experimental import pallas as pl
from jax.experimental.pallas import tpu as pltpu
from jax.sharding import PartitionSpec as P

ROWS = 256
C = 1536
CO = 768
HEADS = 4
DH = 128
REACH = 4
SIDE = 4
SCALE = 1.4426950408889634 / (DH**0.5)
BF = jnp.bfloat16
F32 = jnp.float32

CHUNKS = (
    ((0, 0, 0), (1, 0, 0),),
    ((0, 1, 0), (0, 3, 0), (0, 0, 1), (0, 0, 3),),
    ((1, 1, 0), (1, 3, 0), (1, 0, 1), (1, 0, 3),),
    ((0, 2, 0), (0, 0, 2), (1, 2, 0), (1, 0, 2),),
    ((0, 1, 1), (0, 1, 3), (0, 3, 1), (0, 3, 3),),
    ((1, 1, 1), (1, 1, 3), (1, 3, 1), (1, 3, 3),),
    ((0, 2, 1), (0, 2, 3), (0, 1, 2), (0, 3, 2),),
    ((1, 2, 1), (1, 2, 3), (1, 1, 2), (1, 3, 2),),
    ((0, 2, 2), (1, 2, 2),),
)
ACTS = {
    (0, 0): ((1, 0, 0, 0), (1, 0, 0, 1),),
    (0, 3): ((0, 1, 0, 0), (0, 3, 0, 0), (0, 0, 1, 0), (0, 0, 3, 0),),
    (1, 0): ((0, 1, 0, 1), (0, 3, 0, 1), (0, 0, 1, 1), (0, 0, 3, 1),),
    (1, 3): ((0, 2, 0, 0), (0, 1, 3, 0), (1, 1, 0, 0), (1, 3, 0, 0), (1, 0, 1, 0), (1, 0, 3, 0),),
    (2, 0): ((1, 1, 0, 1), (1, 3, 0, 1), (1, 0, 1, 1), (1, 0, 3, 1),),
    (2, 1): ((0, 1, 1, 0), (0, 3, 3, 0),),
    (2, 3): ((0, 3, 1, 0), (0, 1, 3, 1), (1, 2, 0, 0), (0, 0, 2, 0), (0, 2, 0, 1), (0, 1, 1, 1), (0, 3, 3, 1), (1, 0, 2, 0),),
    (3, 0): ((0, 3, 1, 1), (0, 0, 2, 1), (1, 2, 0, 1), (0, 2, 1, 0), (0, 2, 3, 0), (1, 0, 2, 1),),
    (3, 1): ((0, 1, 2, 0), (0, 1, 2, 1),),
    (3, 3): ((0, 3, 2, 0), (0, 2, 3, 1),),
    (4, 1): ((0, 2, 1, 1), (0, 3, 2, 1),),
    (4, 3): ((1, 1, 3, 0), (1, 1, 1, 0), (1, 3, 3, 0), (1, 3, 1, 0),),
    (5, 0): ((0, 2, 2, 0), (1, 1, 3, 1), (1, 1, 1, 1), (1, 3, 3, 1), (1, 3, 1, 1),),
    (5, 3): ((0, 2, 2, 1),),
    (6, 3): ((1, 2, 1, 0), (1, 2, 3, 0), (1, 1, 2, 0), (1, 3, 2, 0),),
    (7, 0): ((1, 1, 2, 1), (1, 2, 3, 1), (1, 2, 1, 1), (1, 3, 2, 1),),
    (7, 3): ((1, 2, 2, 0),),
    (8, 0): ((1, 2, 2, 1),),
}


ORDER = tuple(b for ch in CHUNKS for b in ch)
SLOT = {b: i for i, b in enumerate(ORDER)}


def nt_dot(a, b):
    return lax.dot_general(a, b, (((1,), (1,)), ((), ())), preferred_element_type=F32)


def nn_dot(a, b):
    return jnp.dot(a, b, preferred_element_type=F32)


def kernel(
    x_hbm, cg_hbm, cw_hbm, cb_hbm, ag_hbm, wq_hbm, wk_hbm, wv_hbm, wo_hbm,
    out_ref,
    x_ref, cg_ref, cw_ref, cb_ref, ag_ref, wq_ref, wkv_ref, wo_ref,
    edge_ref, ext_ref, hid_ref, ain_ref, q_ref, k_ref, v_ref,
    s_ref, acc_ref, stat_ref, att_ref,
    lsem, hsend, hrecv, ssem, rsem,
):
    dp = lax.axis_index("dp")
    me = lax.axis_index("seq")
    core = lax.rem(me, 2)
    chip = me // 2
    cx = chip // SIDE
    cy = lax.rem(chip, SIDE)

    def at(ix, iy, co):
        return (lax.rem(ix, SIDE) * SIDE + lax.rem(iy, SIDE)) * 2 + co

    da_x = 1 - core
    da_y = core
    a_up = at(cx + da_x, cy + da_y, core)
    a_dn = at(cx + da_x * 3, cy + da_y * 3, core)
    b_up = at(cx + da_y, cy + da_x, core)
    b_dn = at(cx + da_y * 3, cy + da_x * 3, core)
    mate = chip * 2 + (1 - core)
    nxt = lax.rem(me + 1, 32)
    prv = lax.rem(me + 31, 32)
    MESH = pl.DeviceIdType.MESH

    def load(src, dst, i):
        return pltpu.make_async_copy(src, dst, lsem.at[i])

    loads = [
        load(x_hbm, x_ref, 0),
        load(cg_hbm, cg_ref, 1),
        load(cw_hbm.at[1], cw_ref.at[1], 2),
        load(cw_hbm.at[0], cw_ref.at[0], 3),
        load(cw_hbm.at[2], cw_ref.at[2], 4),
        load(cb_hbm, cb_ref, 5),
        load(ag_hbm, ag_ref, 6),
        load(wk_hbm, wkv_ref.at[:, 0:DH], 7),
        load(wv_hbm, wkv_ref.at[:, DH : 2 * DH], 8),
        load(wq_hbm, wq_ref, 9),
        load(wo_hbm, wo_ref, 10),
    ]
    for cp in loads:
        cp.start()

    barrier = pltpu.get_barrier_semaphore()
    for who in (nxt, prv, a_up, a_dn, b_up, b_dn, mate):
        pl.semaphore_signal(barrier, inc=1, device_id=(dp, who), device_id_type=MESH)
    pl.semaphore_wait(barrier, 7)

    def remote(src, dst, ss, rs, who):
        return pltpu.make_async_remote_copy(
            src_ref=src, dst_ref=dst, send_sem=ss, recv_sem=rs,
            device_id=(dp, who), device_id_type=MESH,
        )

    halo = [
        remote(x_hbm.at[pl.ds(0, 8)], edge_ref.at[0], hsend.at[0], hrecv.at[0], prv),
        remote(x_hbm.at[pl.ds(ROWS - 8, 8)], edge_ref.at[1], hsend.at[1], hrecv.at[1], nxt),
    ]
    for cp in halo:
        cp.start()

    def norm_rows(wide, gain):
        ms = jnp.sum(wide * wide, axis=-1, keepdims=True) * (1.0 / C)
        return wide * lax.rsqrt(ms + 1e-06) * gain

    loads[0].wait()
    loads[1].wait()
    cgain = cg_ref[...].reshape(1, C)
    for i in range(0, ROWS, 32):
        ext_ref[i : i + 32, :] = norm_rows(x_ref[i : i + 32, :].astype(F32), cgain).astype(BF)

    loads[2].wait()
    for n in range(3):
        cols = slice(n * 256, (n + 1) * 256)
        acc_ref[:, cols] = nn_dot(ext_ref[0:ROWS, :], cw_ref[1, :, cols])

    for cp in halo:
        cp.wait_recv()
    last_ok = jnp.where(me < 31, 1.0, 0.0).astype(F32)
    first_ok = jnp.where(me > 0, 1.0, 0.0).astype(F32)
    edge = jnp.concatenate(
        [edge_ref[0].astype(F32) * last_ok, edge_ref[1].astype(F32) * first_ok], axis=0
    )
    ext_ref[ROWS : ROWS + 16, :] = norm_rows(edge, cgain).astype(BF)

    loads[3].wait()
    loads[4].wait()
    loads[5].wait()
    cbias = cb_ref[...].reshape(1, CO)
    for n in range(3):
        cols = slice(n * 256, (n + 1) * 256)
        up = nn_dot(ext_ref[...], cw_ref[0, :, cols])
        dn = nn_dot(ext_ref[...], cw_ref[2, :, cols])
        up = pltpu.roll(up, REACH, 0)[0:ROWS]
        dn = pltpu.roll(dn, ROWS + 16 - REACH, 0)[0:ROWS]
        z = up + acc_ref[:, cols] + dn + cbias[:, cols]
        g = jax.nn.gelu(z, approximate=True)
        hid_ref[:, cols] = (x_ref[:, cols].astype(F32) + g).astype(BF)

    loads[6].wait()
    again = ag_ref[...].reshape(1, C)
    for i in range(0, ROWS, 32):
        wide = jnp.concatenate([hid_ref[i : i + 32, :], x_ref[i : i + 32, CO:]], axis=1).astype(F32)
        ain_ref[i : i + 32, :] = norm_rows(wide, again).astype(BF)

    loads[7].wait()
    loads[8].wait()
    kv = nn_dot(ain_ref[...], wkv_ref[...])
    k_ref[0] = kv[:, 0:DH].astype(BF)
    v_ref[0] = kv[:, DH : 2 * DH].T.astype(BF)

    sends = []

    def push(part, src, kind, da, db, who):
        ref = v_ref if part else k_ref
        i = len(sends)
        dst = SLOT[(kind, da, db)]
        cp = remote(ref.at[src], ref.at[dst], ssem.at[i], rsem.at[part, dst], who)
        cp.start()
        sends.append(cp)

    def forward(kind, da, db, part):
        if kind:
            return
        src = SLOT[(kind, da, db)]
        if da == 0 and db == 0:
            push(part, src, 0, 1, 0, a_up)
            push(part, src, 0, 3, 0, a_dn)
        if (da, db, part) == (1, 0, 0):
            push(part, src, 0, 2, 0, a_up)
        if (da, db, part) == (3, 0, 1):
            push(part, src, 0, 2, 0, a_dn)
        if db == 0:
            push(part, src, 0, da, 1, b_up)
            push(part, src, 0, da, 3, b_dn)
        if db == 1 and part == 0:
            push(part, src, 0, da, 2, b_up)
        if db == 3 and part == 1:
            push(part, src, 0, da, 2, b_dn)
        push(part, src, 1, da, db, mate)

    def arrive(kind, da, db, part):
        dst = SLOT[(kind, da, db)]
        ref = v_ref if part else k_ref
        remote(ref.at[dst], ref.at[dst], ssem.at[0], rsem.at[part, dst], mate).wait_recv()

    def act(key):
        for msg in ACTS.get(key, ()):
            arrive(*msg)
            forward(*msg)

    forward(0, 0, 0, 0)
    forward(0, 0, 0, 1)

    loads[9].wait()
    qa = nn_dot(ain_ref[...], wq_ref[...]) * SCALE
    for h in range(HEADS):
        q_ref[h * ROWS : (h + 1) * ROWS, :] = qa[:, h * DH : (h + 1) * DH].astype(BF)

    def fold8(x, op):
        return op(x.reshape(x.shape[0] // 8, 8, x.shape[1]), axis=0)

    def scores(slot, r, buf, j):
        s = nt_dot(k_ref[slot], q_ref[r * ROWS : (r + 1) * ROWS, :])
        s_ref[buf, j * 256 : (j + 1) * 256, :] = s
        return fold8(s, jnp.max)

    stat_ref[0:8, :] = jnp.full((8, HEADS * ROWS), -jnp.inf, F32)
    stat_ref[8:16, :] = jnp.zeros((8, HEADS * ROWS), F32)
    acc_ref[0:DH, :] = jnp.zeros((DH, HEADS * ROWS), F32)
    act((0, 0))
    slots = [SLOT[b] for b in CHUNKS[0]]
    top = None
    for j, sl in enumerate(slots):
        t = scores(sl, 0, 0, j)
        top = t if top is None else jnp.maximum(top, t)
    for i in range(len(CHUNKS)):
        slots = [SLOT[b] for b in CHUNKS[i]]
        for r in range(HEADS):
            if (i, r) != (0, 0):
                act((i, r))
            if r < HEADS - 1:
                ahead = [(SLOT[b], r + 1) for b in CHUNKS[i]]
            elif i + 1 < len(CHUNKS):
                ahead = [(SLOT[b], 0) for b in CHUNKS[i + 1]]
            else:
                ahead = []
            buf = (i * HEADS + r) % 2
            lanes = slice(r * ROWS, (r + 1) * ROWS)
            m_old = stat_ref[0:1, lanes]
            m_new = jnp.maximum(m_old, jnp.max(top, axis=0, keepdims=True))
            alpha = jnp.exp2(m_old - m_new)
            stat_ref[0:1, lanes] = m_new
            ntop = None
            total = None
            pv = None
            for j in range(max(len(slots), len(ahead))):
                if j < len(ahead):
                    t = scores(ahead[j][0], ahead[j][1], 1 - buf, j)
                    ntop = t if ntop is None else jnp.maximum(ntop, t)
                if j < len(slots):
                    p = jnp.exp2(s_ref[buf, j * 256 : (j + 1) * 256, :] - m_new)
                    y = fold8(p, jnp.sum)
                    total = y if total is None else total + y
                    z = nn_dot(v_ref[slots[j]], p.astype(BF))
                    pv = z if pv is None else pv + z
            stat_ref[8:16, lanes] = stat_ref[8:16, lanes] * alpha + total
            acc_ref[0:DH, lanes] = acc_ref[0:DH, lanes] * alpha + pv
            top = ntop

    for h in range(HEADS):
        lanes = slice(h * ROWS, (h + 1) * ROWS)
        o = acc_ref[0:DH, lanes] / jnp.sum(stat_ref[8:16, lanes], axis=0, keepdims=True)
        att_ref[:, h * DH : (h + 1) * DH] = o.T.astype(BF)
    loads[10].wait()
    for n in range(6):
        cols = slice(n * 256, (n + 1) * 256)
        base = hid_ref[:, cols] if n < 3 else x_ref[:, cols]
        y = base.astype(F32) + nn_dot(att_ref[...], wo_ref[:, cols])
        out_ref[:, cols] = y.astype(BF)

    for cp in halo + sends:
        cp.wait_send()


N_SENDS = 62


def body(x, cg, cw, cb, ag, wq, wk, wv, wo):
    any_spec = pl.BlockSpec(memory_space=pl.ANY)
    return pl.pallas_call(
        kernel,
        out_shape=jax.ShapeDtypeStruct((ROWS, C), BF),
        in_specs=[any_spec] * 9,
        out_specs=pl.BlockSpec(memory_space=pltpu.VMEM),
        scratch_shapes=[
            pltpu.VMEM((ROWS, C), BF),
            pltpu.VMEM((C,), F32),
            pltpu.VMEM((3, C, CO), BF),
            pltpu.VMEM((CO,), F32),
            pltpu.VMEM((C,), F32),
            pltpu.VMEM((C, HEADS * DH), BF),
            pltpu.VMEM((C, 2 * DH), BF),
            pltpu.VMEM((HEADS * DH, C), BF),
            pltpu.VMEM((2, 8, C), BF),
            pltpu.VMEM((ROWS + 16, C), BF),
            pltpu.VMEM((ROWS, CO), BF),
            pltpu.VMEM((ROWS, C), BF),
            pltpu.VMEM((HEADS * ROWS, DH), BF),
            pltpu.VMEM((32, ROWS, DH), BF),
            pltpu.VMEM((32, DH, ROWS), BF),
            pltpu.VMEM((2, 256 * max(len(c) for c in CHUNKS), ROWS), F32),
            pltpu.VMEM((ROWS, HEADS * ROWS), F32),
            pltpu.VMEM((16, HEADS * ROWS), F32),
            pltpu.VMEM((ROWS, HEADS * DH), BF),
            pltpu.SemaphoreType.DMA((11,)),
            pltpu.SemaphoreType.DMA((2,)),
            pltpu.SemaphoreType.DMA((2,)),
            pltpu.SemaphoreType.DMA((N_SENDS,)),
            pltpu.SemaphoreType.DMA((2, 32)),
        ],
        compiler_params=pltpu.CompilerParams(
            collective_id=0, has_side_effects=True, vmem_limit_bytes=60 << 20
        ),
        name="block",
    )(x, cg, cw, cb, ag, wq, wk, wv, wo)


def solution(mesh):
    placed = (P(("dp", "seq"), None), P(), P(), P(), P(), P(), P(), P(), P())
    return jax.shard_map(
        body, mesh=mesh, in_specs=placed, out_specs=P(("dp", "seq"), None), check_vma=False
    )
```

time: 117 us -> 37.2 us (0.32)
  waiting for transfers between devices: 55.3 us -> 0 us
  Pallas kernels: 0 us -> 35 us
  matrix products: 29.4 us -> 0 us
  between operations: 13.6 us -> 0.01 us
  other arithmetic: 9.62 us -> 0 us
  starting transfers between devices: 6.64 us -> 0 us
    all_gather x1 -> x0, waiting for transfers between devices: 55.1 us -> none  [body(): gathered = lax.all_gather(packed, 'seq', axis=0, tiled=True)]
    pallas_call x0 -> x1, Pallas kernels: none -> 35 us  [body(): pl.pallas_call(kernel, out_shape=jax.ShapeDtypeStruct((ROWS, C), BF), in_...]
    dot_general x15 -> x0, matrix products: 29.4 us -> none  [the longest x4 11.2 us: fold_block(): jnp.einsum('htk,kd->htd', expd.astype(jnp.bfloat16), value_part, preferre...]
    reduce_sum x6 -> x0, other arithmetic: 7.21 us -> none  [the longest x4 5.49 us: fold_block(): totals = totals * factor + jnp.sum(expd, axis=-1)]
    ppermute x2 -> x0, starting transfers between devices: 6.64 us -> none  [the longest x1 4.58 us: padded(): lax.ppermute(tail, axis, [(i, (i + 1) % count) for i in range(ends)])]
    convert_element_type x3 -> x0, other arithmetic: 1.62 us -> none  [the longest x1 1.4 us: body(): normed = normalize(seq_in, conv_gain).astype(jnp.bfloat16)]
  transfers between devices with their start and end apart: 3 -> 0, of which waited for: 2 -> 0; matrix products, arithmetic and copies ran while one was open for 5% -> 0% of each run, Pallas kernels for 0% -> 0%
where the time goes in v1:
time: 37.2 us; the launch traced here: 37.1 us
  Pallas kernels  35 us (94%)
  local copies, waits for them, and re-layouts  2.06 us (6%)
    pallas_call x1, Pallas kernels, body(): pl.pallas_call(kernel, out_shape=jax.ShapeDtypeStruct((ROWS, C), BF), in_...  35 us
    unnamed x1, local copies, waits for them, and re-layouts  2.06 us

profile of v1, /device:TPU:1, one launch (start us, length us, event | category | flops | bytes accessed | tf_op | source)
XLA Modules:
  0.0 37.1 jit_solution(14476070858223894112)
XLA Ops:
  0.0 35.0 %block.1 = bf16[256,1536]{1,0:T(8,128)(2,1)} custom-call(bf16[256,1536]{1,0:T(8,128)(2,1)} %x_hbm.1, f32[1536]{0:T(1024)} %cg_hbm.1, bf16[3,1536,768]{2,1,0:T(8,128)(2,1)} %cw_hbm.1, f32[768]{0:T(1024)} %cb_hbm.1, f32[1536]{0:T(1024)} %ag_hbm.1, bf16[1536,512]{1,0:T(8,128)(2,1)} %wq_hbm.1, bf16[1536,128]{1,0:T(8,128)(2,1)} %wk_hbm.1, ...), custom_call_target="tpu_custom_call" | custom-call | tf_op jit(solution)/shard_map/block/pallas_call | solution.py:299
  35.0 2.1 %copy.11 = bf16[256,1536]{1,0:T(8,128)(2,1)} copy(bf16[256,1536]{1,0:T(8,128)(2,1)} %block.1) | data formatting | bytes 1572864

commit v2 on v1

--- a/solution.py
+++ b/solution.py
@@ -16,36 +16,34 @@
 BF = jnp.bfloat16
 F32 = jnp.float32
 
+FAR = (2,)
+FAR_A = True
+LATE_B = True
 CHUNKS = (
     ((0, 0, 0), (1, 0, 0),),
-    ((0, 1, 0), (0, 3, 0), (0, 0, 1), (0, 0, 3),),
-    ((1, 1, 0), (1, 3, 0), (1, 0, 1), (1, 0, 3),),
-    ((0, 2, 0), (0, 0, 2), (1, 2, 0), (1, 0, 2),),
-    ((0, 1, 1), (0, 1, 3), (0, 3, 1), (0, 3, 3),),
-    ((1, 1, 1), (1, 1, 3), (1, 3, 1), (1, 3, 3),),
-    ((0, 2, 1), (0, 2, 3), (0, 1, 2), (0, 3, 2),),
-    ((1, 2, 1), (1, 2, 3), (1, 1, 2), (1, 3, 2),),
-    ((0, 2, 2), (1, 2, 2),),
+    ((0, 1, 0), (0, 3, 0), (0, 2, 0),),
+    ((1, 3, 0), (1, 1, 0), (0, 0, 1),),
+    ((0, 0, 3), (1, 2, 0), (1, 0, 3),),
+    ((1, 0, 1), (0, 3, 3), (0, 1, 3),),
+    ((0, 3, 1), (1, 3, 3), (0, 1, 1),),
+    ((0, 2, 3), (1, 3, 1), (1, 1, 3),),
+    ((0, 2, 1), (1, 1, 1), (1, 2, 3),),
+    ((0, 0, 2), (0, 2, 2), (1, 2, 1),),
+    ((1, 0, 2), (0, 1, 2), (0, 3, 2),),
+    ((1, 2, 2), (1, 3, 2), (1, 1, 2),),
 )
 ACTS = {
     (0, 0): ((1, 0, 0, 0), (1, 0, 0, 1),),
-    (0, 3): ((0, 1, 0, 0), (0, 3, 0, 0), (0, 0, 1, 0), (0, 0, 3, 0),),
-    (1, 0): ((0, 1, 0, 1), (0, 3, 0, 1), (0, 0, 1, 1), (0, 0, 3, 1),),
-    (1, 3): ((0, 2, 0, 0), (0, 1, 3, 0), (1, 1, 0, 0), (1, 3, 0, 0), (1, 0, 1, 0), (1, 0, 3, 0),),
-    (2, 0): ((1, 1, 0, 1), (1, 3, 0, 1), (1, 0, 1, 1), (1, 0, 3, 1),),
-    (2, 1): ((0, 1, 1, 0), (0, 3, 3, 0),),
-    (2, 3): ((0, 3, 1, 0), (0, 1, 3, 1), (1, 2, 0, 0), (0, 0, 2, 0), (0, 2, 0, 1), (0, 1, 1, 1), (0, 3, 3, 1), (1, 0, 2, 0),),
-    (3, 0): ((0, 3, 1, 1), (0, 0, 2, 1), (1, 2, 0, 1), (0, 2, 1, 0), (0, 2, 3, 0), (1, 0, 2, 1),),
-    (3, 1): ((0, 1, 2, 0), (0, 1, 2, 1),),
-    (3, 3): ((0, 3, 2, 0), (0, 2, 3, 1),),
-    (4, 1): ((0, 2, 1, 1), (0, 3, 2, 1),),
-    (4, 3): ((1, 1, 3, 0), (1, 1, 1, 0), (1, 3, 3, 0), (1, 3, 1, 0),),
-    (5, 0): ((0, 2, 2, 0), (1, 1, 3, 1), (1, 1, 1, 1), (1, 3, 3, 1), (1, 3, 1, 1),),
-    (5, 3): ((0, 2, 2, 1),),
-    (6, 3): ((1, 2, 1, 0), (1, 2, 3, 0), (1, 1, 2, 0), (1, 3, 2, 0),),
-    (7, 0): ((1, 1, 2, 1), (1, 2, 3, 1), (1, 2, 1, 1), (1, 3, 2, 1),),
-    (7, 3): ((1, 2, 2, 0),),
-    (8, 0): ((1, 2, 2, 1),),
+    (0, 3): ((0, 1, 0, 0), (0, 3, 0, 0), (0, 2, 0, 0), (0, 0, 1, 0), (0, 0, 3, 0), (0, 3, 0, 1), (0, 1, 0, 1), (0, 2, 0, 1),),
+    (1, 3): ((0, 0, 3, 1), (0, 0, 1, 1), (1, 1, 0, 0), (1, 3, 0, 0), (1, 3, 0, 1), (1, 1, 0, 1),),
+    (2, 3): ((0, 1, 1, 0), (0, 1, 3, 0), (0, 3, 1, 0), (0, 3, 3, 0), (1, 2, 0, 0), (1, 0, 3, 0), (1, 2, 0, 1), (1, 0, 3, 1),),
+    (3, 3): ((0, 2, 1, 0), (0, 2, 3, 0), (1, 0, 1, 0), (1, 0, 1, 1), (0, 2, 2, 0), (0, 0, 2, 0), (0, 3, 3, 1), (0, 3, 1, 1), (0, 1, 3, 1),),
+    (4, 3): ((0, 1, 1, 1), (0, 2, 3, 1), (1, 3, 3, 0), (1, 3, 3, 1),),
+    (5, 3): ((0, 2, 1, 1), (1, 1, 3, 0), (1, 3, 1, 0), (1, 3, 1, 1), (1, 1, 3, 1),),
+    (6, 3): ((0, 0, 2, 1), (0, 2, 2, 1), (0, 1, 2, 0), (0, 3, 2, 1), (1, 1, 1, 0), (1, 2, 3, 0), (1, 1, 1, 1), (1, 2, 3, 1),),
+    (7, 3): ((0, 3, 2, 0), (0, 1, 2, 1), (1, 2, 1, 0), (1, 2, 1, 1),),
+    (8, 3): ((1, 0, 2, 0), (1, 0, 2, 1),),
+    (9, 3): ((1, 2, 2, 0), (1, 2, 2, 1), (1, 1, 2, 0), (1, 3, 2, 1), (1, 3, 2, 0), (1, 1, 2, 1),),
 }
 
 
@@ -85,6 +83,8 @@
     a_dn = at(cx + da_x * 3, cy + da_y * 3, core)
     b_up = at(cx + da_y, cy + da_x, core)
     b_dn = at(cx + da_y * 3, cy + da_x * 3, core)
+    a_far = at(cx + da_x * 2, cy + da_y * 2, core)
+    b_far = at(cx + da_y * 2, cy + da_x * 2, core)
     mate = chip * 2 + (1 - core)
     nxt = lax.rem(me + 1, 32)
     prv = lax.rem(me + 31, 32)
@@ -93,12 +93,15 @@
     def load(src, dst, i):
         return pltpu.make_async_copy(src, dst, lsem.at[i])
 
+    def wcols(n):
+        return slice(n * 256, (n + 1) * 256)
+
     loads = [
         load(x_hbm, x_ref, 0),
         load(cg_hbm, cg_ref, 1),
-        load(cw_hbm.at[1], cw_ref.at[1], 2),
-        load(cw_hbm.at[0], cw_ref.at[0], 3),
-        load(cw_hbm.at[2], cw_ref.at[2], 4),
+        load(cw_hbm.at[:, :, wcols(0)], cw_ref.at[:, :, wcols(0)], 2),
+        load(cw_hbm.at[:, :, wcols(1)], cw_ref.at[:, :, wcols(1)], 3),
+        load(cw_hbm.at[:, :, wcols(2)], cw_ref.at[:, :, wcols(2)], 4),
         load(cb_hbm, cb_ref, 5),
         load(ag_hbm, ag_ref, 6),
         load(wk_hbm, wkv_ref.at[:, 0:DH], 7),
@@ -106,13 +109,12 @@
         load(wq_hbm, wq_ref, 9),
         load(wo_hbm, wo_ref, 10),
     ]
-    for cp in loads:
+    for cp in loads[:7]:
         cp.start()
 
     barrier = pltpu.get_barrier_semaphore()
-    for who in (nxt, prv, a_up, a_dn, b_up, b_dn, mate):
+    for who in (nxt, prv, a_up, a_dn, b_up, b_dn, a_far, b_far, mate):
         pl.semaphore_signal(barrier, inc=1, device_id=(dp, who), device_id_type=MESH)
-    pl.semaphore_wait(barrier, 7)
 
     def remote(src, dst, ss, rs, who):
         return pltpu.make_async_remote_copy(
@@ -121,12 +123,9 @@
         )
 
     halo = [
-        remote(x_hbm.at[pl.ds(0, 8)], edge_ref.at[0], hsend.at[0], hrecv.at[0], prv),
-        remote(x_hbm.at[pl.ds(ROWS - 8, 8)], edge_ref.at[1], hsend.at[1], hrecv.at[1], nxt),
+        remote(x_ref.at[pl.ds(0, 8)], edge_ref.at[0], hsend.at[0], hrecv.at[0], prv),
+        remote(x_ref.at[pl.ds(ROWS - 8, 8)], edge_ref.at[1], hsend.at[1], hrecv.at[1], nxt),
     ]
-    for cp in halo:
-        cp.start()
-
     def norm_rows(wide, gain):
         ms = jnp.sum(wide * wide, axis=-1, keepdims=True) * (1.0 / C)
         return wide * lax.rsqrt(ms + 1e-06) * gain
@@ -137,11 +136,24 @@
     for i in range(0, ROWS, 32):
         ext_ref[i : i + 32, :] = norm_rows(x_ref[i : i + 32, :].astype(F32), cgain).astype(BF)
 
-    loads[2].wait()
+    pl.semaphore_wait(barrier, 9)
+    for cp in halo:
+        cp.start()
+    for cp in loads[7:]:
+        cp.start()
+    ring8 = lax.broadcasted_iota(jnp.int32, (8, 256), 0)
     for n in range(3):
-        cols = slice(n * 256, (n + 1) * 256)
-        acc_ref[:, cols] = nn_dot(ext_ref[0:ROWS, :], cw_ref[1, :, cols])
-
+        cols = wcols(n)
+        loads[2 + n].wait()
+        mid = nn_dot(ext_ref[0:ROWS, :], cw_ref[1, :, cols])
+        up = pltpu.roll(nn_dot(ext_ref[0:ROWS, :], cw_ref[0, :, cols]), REACH, 0)
+        dn = pltpu.roll(nn_dot(ext_ref[0:ROWS, :], cw_ref[2, :, cols]), ROWS - REACH, 0)
+        up = jnp.concatenate([jnp.where(ring8 < REACH, 0.0, up[0:8]), up[8:]], axis=0)
+        dn = jnp.concatenate([dn[0:-8], jnp.where(ring8 < REACH, dn[-8:], 0.0)], axis=0)
+        acc_ref[:, cols] = up + mid + dn
+
+    loads[5].wait()
+    cbias = cb_ref[...].reshape(1, CO)
     for cp in halo:
         cp.wait_recv()
     last_ok = jnp.where(me < 31, 1.0, 0.0).astype(F32)
@@ -149,20 +161,20 @@
     edge = jnp.concatenate(
         [edge_ref[0].astype(F32) * last_ok, edge_ref[1].astype(F32) * first_ok], axis=0
     )
-    ext_ref[ROWS : ROWS + 16, :] = norm_rows(edge, cgain).astype(BF)
-
-    loads[3].wait()
-    loads[4].wait()
-    loads[5].wait()
-    cbias = cb_ref[...].reshape(1, CO)
+    edge = norm_rows(edge, cgain).astype(BF)
     for n in range(3):
-        cols = slice(n * 256, (n + 1) * 256)
-        up = nn_dot(ext_ref[...], cw_ref[0, :, cols])
-        dn = nn_dot(ext_ref[...], cw_ref[2, :, cols])
-        up = pltpu.roll(up, REACH, 0)[0:ROWS]
-        dn = pltpu.roll(dn, ROWS + 16 - REACH, 0)[0:ROWS]
-        z = up + acc_ref[:, cols] + dn + cbias[:, cols]
-        g = jax.nn.gelu(z, approximate=True)
+        cols = wcols(n)
+        up = pltpu.roll(nn_dot(edge, cw_ref[0, :, cols])[8:16], REACH, 0)
+        dn = pltpu.roll(nn_dot(edge, cw_ref[2, :, cols])[0:8], REACH, 0)
+        z = jnp.concatenate(
+            [
+                acc_ref[0:8, cols] + jnp.where(ring8 < REACH, up, 0.0),
+                acc_ref[8 : ROWS - 8, cols],
+                acc_ref[ROWS - 8 : ROWS, cols] + jnp.where(ring8 < REACH, 0.0, dn),
+            ],
+            axis=0,
+        )
+        g = jax.nn.gelu(z + cbias[:, cols], approximate=True)
         hid_ref[:, cols] = (x_ref[:, cols].astype(F32) + g).astype(BF)
 
     loads[6].wait()
@@ -187,25 +199,34 @@
         cp.start()
         sends.append(cp)
 
-    def forward(kind, da, db, part):
+    def forward(kind, da, db, part, legs="ABM"):
         if kind:
             return
         src = SLOT[(kind, da, db)]
-        if da == 0 and db == 0:
-            push(part, src, 0, 1, 0, a_up)
-            push(part, src, 0, 3, 0, a_dn)
-        if (da, db, part) == (1, 0, 0):
-            push(part, src, 0, 2, 0, a_up)
-        if (da, db, part) == (3, 0, 1):
-            push(part, src, 0, 2, 0, a_dn)
-        if db == 0:
-            push(part, src, 0, da, 1, b_up)
-            push(part, src, 0, da, 3, b_dn)
-        if db == 1 and part == 0:
-            push(part, src, 0, da, 2, b_up)
-        if db == 3 and part == 1:
-            push(part, src, 0, da, 2, b_dn)
-        push(part, src, 1, da, db, mate)
+        turn = -1 if part else 1
+        if "A" in legs:
+            if da == 0 and db == 0:
+                for to, who in ((1, a_up), (3, a_dn))[::turn]:
+                    push(part, src, 0, to, 0, who)
+                if FAR_A:
+                    push(part, src, 0, 2, 0, a_far)
+            if not FAR_A and (da, db, part) == (1, 0, 0):
+                push(part, src, 0, 2, 0, a_up)
+            if not FAR_A and (da, db, part) == (3, 0, 1):
+                push(part, src, 0, 2, 0, a_dn)
+        if "B" in legs:
+            if db == 0:
+                for to, who in ((1, b_up), (3, b_dn))[::turn]:
+                    push(part, src, 0, da, to, who)
+                if da in FAR:
+                    push(part, src, 0, da, 2, b_far)
+            elif da not in FAR:
+                if db == 1 and part == 0:
+                    push(part, src, 0, da, 2, b_up)
+                if db == 3 and part == 1:
+                    push(part, src, 0, da, 2, b_dn)
+        if "M" in legs:
+            push(part, src, 1, da, db, mate)
 
     def arrive(kind, da, db, part):
         dst = SLOT[(kind, da, db)]
@@ -217,13 +238,17 @@
             arrive(*msg)
             forward(*msg)
 
-    forward(0, 0, 0, 0)
-    forward(0, 0, 0, 1)
+    for part in (0, 1):
+        forward(0, 0, 0, part, "AM" if LATE_B else "ABM")
 
     loads[9].wait()
     qa = nn_dot(ain_ref[...], wq_ref[...]) * SCALE
     for h in range(HEADS):
         q_ref[h * ROWS : (h + 1) * ROWS, :] = qa[:, h * DH : (h + 1) * DH].astype(BF)
+
+    if LATE_B:
+        for part in (0, 1):
+            forward(0, 0, 0, part, "B")
 
     def fold8(x, op):
         return op(x.reshape(x.shape[0] // 8, 8, x.shape[1]), axis=0)
@@ -291,9 +316,6 @@
         cp.wait_send()
 
 
-N_SENDS = 62
-
-
 def body(x, cg, cw, cb, ag, wq, wk, wv, wo):
     any_spec = pl.BlockSpec(memory_space=pl.ANY)
     return pl.pallas_call(
@@ -311,7 +333,7 @@
             pltpu.VMEM((C, 2 * DH), BF),
             pltpu.VMEM((HEADS * DH, C), BF),
             pltpu.VMEM((2, 8, C), BF),
-            pltpu.VMEM((ROWS + 16, C), BF),
+            pltpu.VMEM((ROWS, C), BF),
             pltpu.VMEM((ROWS, CO), BF),
             pltpu.VMEM((ROWS, C), BF),
             pltpu.VMEM((HEADS * ROWS, DH), BF),
@@ -324,14 +346,14 @@
             pltpu.SemaphoreType.DMA((11,)),
             pltpu.SemaphoreType.DMA((2,)),
             pltpu.SemaphoreType.DMA((2,)),
-            pltpu.SemaphoreType.DMA((N_SENDS,)),
+            pltpu.SemaphoreType.DMA((62,)),
             pltpu.SemaphoreType.DMA((2, 32)),
         ],
         compiler_params=pltpu.CompilerParams(
-            collective_id=0, has_side_effects=True, vmem_limit_bytes=60 << 20
+            collective_id=0, has_side_effects=True, vmem_limit_bytes=40 << 20
         ),
         name="block",
-    )(x, cg, cw, cb, ag, wq, wk, wv, wo)
+    )(*(pltpu.with_memory_space_constraint(t, pltpu.HBM) for t in (x, cg, cw, cb, ag, wq, wk, wv, wo)))
 
 
 def solution(mesh):

time: 37.2 us -> 34.7 us (0.933)
  Pallas kernels: 35 us -> 33.8 us
  local copies, waits for them, and re-layouts: 2.06 us -> 0.88 us
    pallas_call x1, Pallas kernels: 35 us -> 33.8 us  [body(): pl.pallas_call(kernel, out_shape=jax.ShapeDtypeStruct((ROWS, C), BF), in_...]
    unnamed x1, local copies, waits for them, and re-layouts: 2.06 us -> 0.88 us
where the time goes in v2:
time: 34.7 us
  Pallas kernels  33.8 us (97%)
  local copies, waits for them, and re-layouts  0.88 us (3%)
    pallas_call x1, Pallas kernels, body(): pl.pallas_call(kernel, out_shape=jax.ShapeDtypeStruct((ROWS, C), BF), in_...  33.8 us
    unnamed x1, local copies, waits for them, and re-layouts  0.88 us

profile of v2, /device:TPU:1, one launch (start us, length us, event | category | flops | bytes accessed | tf_op | source)
XLA Modules:
  0.0 34.7 jit_solution(3132046095546267522)
XLA Ops:
  0.0 33.8 %block.1 = bf16[256,1536]{1,0:T(8,128)(2,1)S(1)} custom-call(bf16[256,1536]{1,0:T(8,128)(2,1)} %x_hbm.1, f32[1536]{0:T(1024)} %cg_hbm.1, bf16[3,1536,768]{2,1,0:T(8,128)(2,1)} %cw_hbm.1, f32[768]{0:T(1024)} %cb_hbm.1, f32[1536]{0:T(1024)} %ag_hbm.1, bf16[1536,512]{1,0:T(8,128)(2,1)} %wq_hbm.1, bf16[1536,128]{1,0:T(8,128)(2,1)} %wk_hbm.1, ...), custom_call_target="tpu_custom_call" | custom-call | tf_op jit(solution)/shard_map/block/pallas_call | solution.py:321
  33.8 0.9 %copy.11 = bf16[256,1536]{1,0:T(8,128)(2,1)} copy(bf16[256,1536]{1,0:T(8,128)(2,1)S(1)} %block.1) | data formatting | bytes 1572864

commit v3 on v2

--- a/solution.py
+++ b/solution.py
@@ -6,6 +6,7 @@
 from jax.sharding import PartitionSpec as P
 
 ROWS = 256
+BULK = 240
 C = 1536
 CO = 768
 HEADS = 4
@@ -17,37 +18,39 @@
 F32 = jnp.float32
 
 FAR = (2,)
-FAR_A = True
-LATE_B = True
+FAR_A = False
+LATE_B = False
+EDGE_AT = (3, 7, 9)
 CHUNKS = (
     ((0, 0, 0), (1, 0, 0),),
-    ((0, 1, 0), (0, 3, 0), (0, 2, 0),),
-    ((1, 3, 0), (1, 1, 0), (0, 0, 1),),
-    ((0, 0, 3), (1, 2, 0), (1, 0, 3),),
-    ((1, 0, 1), (0, 3, 3), (0, 1, 3),),
+    ((0, 1, 0), (0, 3, 0), (0, 0, 1),),
+    ((0, 0, 3), (1, 3, 0), (1, 1, 0),),
+    ((1, 0, 3), (1, 0, 1), (0, 2, 0),),
+    ((0, 3, 3), (1, 2, 0), (0, 1, 3),),
     ((0, 3, 1), (1, 3, 3), (0, 1, 1),),
-    ((0, 2, 3), (1, 3, 1), (1, 1, 3),),
-    ((0, 2, 1), (1, 1, 1), (1, 2, 3),),
-    ((0, 0, 2), (0, 2, 2), (1, 2, 1),),
-    ((1, 0, 2), (0, 1, 2), (0, 3, 2),),
-    ((1, 2, 2), (1, 3, 2), (1, 1, 2),),
+    ((0, 0, 2), (1, 3, 1), (1, 1, 3),),
+    ((1, 1, 1), (1, 0, 2), (0, 2, 3),),
+    ((0, 2, 1), (0, 3, 2), (1, 2, 3),),
+    ((0, 1, 2), (0, 2, 2), (1, 2, 1),),
+    ((2, 0, 0), (2, 1, 0),),
+    ((1, 3, 2), (1, 1, 2), (1, 2, 2),),
 )
 ACTS = {
     (0, 0): ((1, 0, 0, 0), (1, 0, 0, 1),),
-    (0, 3): ((0, 1, 0, 0), (0, 3, 0, 0), (0, 2, 0, 0), (0, 0, 1, 0), (0, 0, 3, 0), (0, 3, 0, 1), (0, 1, 0, 1), (0, 2, 0, 1),),
-    (1, 3): ((0, 0, 3, 1), (0, 0, 1, 1), (1, 1, 0, 0), (1, 3, 0, 0), (1, 3, 0, 1), (1, 1, 0, 1),),
-    (2, 3): ((0, 1, 1, 0), (0, 1, 3, 0), (0, 3, 1, 0), (0, 3, 3, 0), (1, 2, 0, 0), (1, 0, 3, 0), (1, 2, 0, 1), (1, 0, 3, 1),),
-    (3, 3): ((0, 2, 1, 0), (0, 2, 3, 0), (1, 0, 1, 0), (1, 0, 1, 1), (0, 2, 2, 0), (0, 0, 2, 0), (0, 3, 3, 1), (0, 3, 1, 1), (0, 1, 3, 1),),
-    (4, 3): ((0, 1, 1, 1), (0, 2, 3, 1), (1, 3, 3, 0), (1, 3, 3, 1),),
-    (5, 3): ((0, 2, 1, 1), (1, 1, 3, 0), (1, 3, 1, 0), (1, 3, 1, 1), (1, 1, 3, 1),),
-    (6, 3): ((0, 0, 2, 1), (0, 2, 2, 1), (0, 1, 2, 0), (0, 3, 2, 1), (1, 1, 1, 0), (1, 2, 3, 0), (1, 1, 1, 1), (1, 2, 3, 1),),
-    (7, 3): ((0, 3, 2, 0), (0, 1, 2, 1), (1, 2, 1, 0), (1, 2, 1, 1),),
-    (8, 3): ((1, 0, 2, 0), (1, 0, 2, 1),),
-    (9, 3): ((1, 2, 2, 0), (1, 2, 2, 1), (1, 1, 2, 0), (1, 3, 2, 1), (1, 3, 2, 0), (1, 1, 2, 1),),
+    (0, 3): ((0, 1, 0, 0), (0, 3, 0, 0), (0, 0, 1, 0), (0, 0, 3, 0), (0, 3, 0, 1), (0, 1, 0, 1), (0, 0, 3, 1), (0, 0, 1, 1),),
+    (1, 3): ((1, 1, 0, 0), (1, 3, 0, 0), (1, 3, 0, 1), (1, 1, 0, 1),),
+    (2, 3): ((0, 2, 0, 0), (0, 1, 3, 0), (0, 1, 1, 0), (0, 3, 3, 0), (1, 0, 1, 0), (1, 0, 3, 0), (1, 0, 3, 1), (1, 0, 1, 1), (0, 3, 1, 0), (0, 2, 0, 1),),
+    (3, 3): ((0, 0, 2, 0), (0, 3, 3, 1), (1, 2, 0, 0), (1, 2, 0, 1), (0, 3, 1, 1), (0, 1, 3, 1),),
+    (4, 3): ((0, 1, 1, 1), (0, 0, 2, 1), (1, 3, 3, 0), (1, 3, 3, 1),),
+    (5, 3): ((0, 2, 1, 0), (0, 2, 3, 0), (1, 1, 3, 0), (1, 3, 1, 0), (1, 3, 1, 1), (1, 1, 3, 1),),
+    (6, 3): ((0, 2, 2, 0), (0, 1, 2, 0), (0, 2, 3, 1), (1, 1, 1, 0), (1, 0, 2, 0), (1, 1, 1, 1), (1, 0, 2, 1),),
+    (7, 3): ((0, 3, 2, 0), (1, 2, 3, 0), (0, 2, 1, 1), (0, 3, 2, 1), (1, 2, 3, 1),),
+    (8, 3): ((0, 1, 2, 1), (0, 2, 2, 1), (1, 2, 1, 0), (1, 2, 1, 1),),
+    (10, 3): ((1, 2, 2, 0), (1, 1, 2, 0), (1, 3, 2, 0), (1, 3, 2, 1), (1, 1, 2, 1), (1, 2, 2, 1),),
 }
 
 
-ORDER = tuple(b for ch in CHUNKS for b in ch)
+ORDER = tuple(b for ch in CHUNKS for b in ch if b[0] < 2)
 SLOT = {b: i for i, b in enumerate(ORDER)}
 
 
@@ -64,8 +67,8 @@
     out_ref,
     x_ref, cg_ref, cw_ref, cb_ref, ag_ref, wq_ref, wkv_ref, wo_ref,
     edge_ref, ext_ref, hid_ref, ain_ref, q_ref, k_ref, v_ref,
-    s_ref, acc_ref, stat_ref, att_ref,
-    lsem, hsend, hrecv, ssem, rsem,
+    s_ref, acc_ref, stat_ref, att_ref, qf_ref, he_ref, e_ref, ve_ref,
+    lsem, hsend, hrecv, ssem, rsem, esend, erecv,
 ):
     dp = lax.axis_index("dp")
     me = lax.axis_index("seq")
@@ -154,27 +157,9 @@
 
     loads[5].wait()
     cbias = cb_ref[...].reshape(1, CO)
-    for cp in halo:
-        cp.wait_recv()
-    last_ok = jnp.where(me < 31, 1.0, 0.0).astype(F32)
-    first_ok = jnp.where(me > 0, 1.0, 0.0).astype(F32)
-    edge = jnp.concatenate(
-        [edge_ref[0].astype(F32) * last_ok, edge_ref[1].astype(F32) * first_ok], axis=0
-    )
-    edge = norm_rows(edge, cgain).astype(BF)
     for n in range(3):
         cols = wcols(n)
-        up = pltpu.roll(nn_dot(edge, cw_ref[0, :, cols])[8:16], REACH, 0)
-        dn = pltpu.roll(nn_dot(edge, cw_ref[2, :, cols])[0:8], REACH, 0)
-        z = jnp.concatenate(
-            [
-                acc_ref[0:8, cols] + jnp.where(ring8 < REACH, up, 0.0),
-                acc_ref[8 : ROWS - 8, cols],
-                acc_ref[ROWS - 8 : ROWS, cols] + jnp.where(ring8 < REACH, 0.0, dn),
-            ],
-            axis=0,
-        )
-        g = jax.nn.gelu(z + cbias[:, cols], approximate=True)
+        g = jax.nn.gelu(acc_ref[:, cols] + cbias[:, cols], approximate=True)
         hid_ref[:, cols] = (x_ref[:, cols].astype(F32) + g).astype(BF)
 
     loads[6].wait()
@@ -186,8 +171,9 @@
     loads[7].wait()
     loads[8].wait()
     kv = nn_dot(ain_ref[...], wkv_ref[...])
-    k_ref[0] = kv[:, 0:DH].astype(BF)
-    v_ref[0] = kv[:, DH : 2 * DH].T.astype(BF)
+    k_ref[0] = kv[8 : ROWS - 8, 0:DH].astype(BF)
+    vals = jnp.concatenate([kv[8 : ROWS - 8, DH : 2 * DH], jnp.zeros((16, DH), F32)], axis=0)
+    v_ref[0] = vals.T.astype(BF)
 
     sends = []
 
@@ -242,40 +228,122 @@
         forward(0, 0, 0, part, "AM" if LATE_B else "ABM")
 
     loads[9].wait()
-    qa = nn_dot(ain_ref[...], wq_ref[...]) * SCALE
-    for h in range(HEADS):
-        q_ref[h * ROWS : (h + 1) * ROWS, :] = qa[:, h * DH : (h + 1) * DH].astype(BF)
+    qf_ref[...] = nn_dot(ain_ref[...], wq_ref[...]) * SCALE
 
     if LATE_B:
         for part in (0, 1):
             forward(0, 0, 0, part, "B")
 
+    for cp in halo:
+        cp.wait_recv()
+    last_ok = jnp.where(me < 31, 1.0, 0.0).astype(F32)
+    first_ok = jnp.where(me > 0, 1.0, 0.0).astype(F32)
+    edge = jnp.concatenate(
+        [edge_ref[0].astype(F32) * last_ok, edge_ref[1].astype(F32) * first_ok], axis=0
+    )
+    edge = norm_rows(edge, cgain).astype(BF)
+
+    def ends(v):
+        return jnp.concatenate([v[0:8], v[-8:]], axis=0)
+
+    x_ends = ends(jnp.concatenate([x_ref[0:16, :], x_ref[ROWS - 16 : ROWS, :]], axis=0).astype(F32))
+    for n in range(3):
+        cols = wcols(n)
+        up = pltpu.roll(nn_dot(edge, cw_ref[0, :, cols])[8:16], REACH, 0)
+        dn = pltpu.roll(nn_dot(edge, cw_ref[2, :, cols])[0:8], REACH, 0)
+        z = jnp.concatenate(
+            [
+                acc_ref[0:8, cols] + jnp.where(ring8 < REACH, up, 0.0),
+                acc_ref[ROWS - 8 : ROWS, cols] + jnp.where(ring8 < REACH, 0.0, dn),
+            ],
+            axis=0,
+        )
+        g = jax.nn.gelu(z + cbias[:, cols], approximate=True)
+        he_ref[:, cols] = (x_ends[:, cols] + g).astype(BF).astype(F32)
+    ain_e = norm_rows(
+        jnp.concatenate([he_ref[...], x_ends[:, CO:]], axis=1), again
+    ).astype(BF)
+    e_ref[0, 0, 0] = nn_dot(ain_e, wkv_ref[...]).astype(BF)
+
+    def edge_copy(i, src, dst, who):
+        return remote(e_ref.at[src], e_ref.at[dst], esend.at[i], erecv.at[i], who)
+
+    edges = [
+        edge_copy(0, (0, 0, 0), (0, 0, 1), a_up),
+        edge_copy(1, (0, 0, 0), (0, 0, 3), a_dn),
+        edge_copy(2, (0, 0, 0), (0, 0, 2), a_far),
+        edge_copy(3, (0, 0), (0, 1), b_up),
+        edge_copy(4, (0, 0), (0, 3), b_dn),
+        edge_copy(5, (0, 0), (0, 2), b_far),
+        edge_copy(6, (0,), (1,), mate),
+    ]
+    for cp in edges[0:3]:
+        cp.start()
+    q_e = nn_dot(ain_e, wq_ref[...]) * SCALE
+    for h in range(HEADS):
+        lanes = slice(h * DH, (h + 1) * DH)
+        full = jnp.concatenate(
+            [q_e[0:8, lanes], qf_ref[8 : ROWS - 8, lanes], q_e[8:16, lanes]], axis=0
+        )
+        q_ref[h * ROWS : (h + 1) * ROWS, :] = full.astype(BF)
+
+    def edge_part(kind, lanes):
+        return e_ref[kind, :, :, :, lanes].reshape(256, DH)
+
+    def edge_step(i):
+        if i == EDGE_AT[0]:
+            for cp in edges[0:3]:
+                cp.wait_recv()
+            for cp in edges[3:6]:
+                cp.start()
+        if i == EDGE_AT[1]:
+            for cp in edges[3:6]:
+                cp.wait_recv()
+            edges[6].start()
+            ve_ref[0] = edge_part(0, slice(DH, 2 * DH)).astype(F32).T.astype(BF)
+        if i == EDGE_AT[2]:
+            edges[6].wait_recv()
+            ve_ref[1] = edge_part(1, slice(DH, 2 * DH)).astype(F32).T.astype(BF)
+
     def fold8(x, op):
         return op(x.reshape(x.shape[0] // 8, 8, x.shape[1]), axis=0)
 
-    def scores(slot, r, buf, j):
-        s = nt_dot(k_ref[slot], q_ref[r * ROWS : (r + 1) * ROWS, :])
-        s_ref[buf, j * 256 : (j + 1) * 256, :] = s
+    def scores(block, r, buf, j):
+        keys = edge_part(block[1], slice(0, DH)) if block[0] == 2 else k_ref[SLOT[block]]
+        s = nt_dot(keys, q_ref[r * ROWS : (r + 1) * ROWS, :])
+        s_ref[buf, j * 256 : j * 256 + s.shape[0], :] = s
         return fold8(s, jnp.max)
+
+    def values(block, p):
+        p = p.astype(BF)
+        if block[0] == 2:
+            return nn_dot(ve_ref[block[1]], p)
+        p = jnp.concatenate([p, jnp.zeros((16, ROWS), BF)], axis=0)
+        return nn_dot(v_ref[SLOT[block]], p)
+
+    def extent(block):
+        return 256 if block[0] == 2 else BULK
 
     stat_ref[0:8, :] = jnp.full((8, HEADS * ROWS), -jnp.inf, F32)
     stat_ref[8:16, :] = jnp.zeros((8, HEADS * ROWS), F32)
     acc_ref[0:DH, :] = jnp.zeros((DH, HEADS * ROWS), F32)
     act((0, 0))
-    slots = [SLOT[b] for b in CHUNKS[0]]
+    slots = CHUNKS[0]
     top = None
     for j, sl in enumerate(slots):
         t = scores(sl, 0, 0, j)
         top = t if top is None else jnp.maximum(top, t)
     for i in range(len(CHUNKS)):
-        slots = [SLOT[b] for b in CHUNKS[i]]
+        slots = CHUNKS[i]
         for r in range(HEADS):
             if (i, r) != (0, 0):
                 act((i, r))
+            if r == HEADS - 1:
+                edge_step(i)
             if r < HEADS - 1:
-                ahead = [(SLOT[b], r + 1) for b in CHUNKS[i]]
+                ahead = [(b, r + 1) for b in CHUNKS[i]]
             elif i + 1 < len(CHUNKS):
-                ahead = [(SLOT[b], 0) for b in CHUNKS[i + 1]]
+                ahead = [(b, 0) for b in CHUNKS[i + 1]]
             else:
                 ahead = []
             buf = (i * HEADS + r) % 2
@@ -292,10 +360,10 @@
                     t = scores(ahead[j][0], ahead[j][1], 1 - buf, j)
                     ntop = t if ntop is None else jnp.maximum(ntop, t)
                 if j < len(slots):
-                    p = jnp.exp2(s_ref[buf, j * 256 : (j + 1) * 256, :] - m_new)
+                    p = jnp.exp2(s_ref[buf, j * 256 : j * 256 + extent(slots[j]), :] - m_new)
                     y = fold8(p, jnp.sum)
                     total = y if total is None else total + y
-                    z = nn_dot(v_ref[slots[j]], p.astype(BF))
+                    z = values(slots[j], p)
                     pv = z if pv is None else pv + z
             stat_ref[8:16, lanes] = stat_ref[8:16, lanes] * alpha + total
             acc_ref[0:DH, lanes] = acc_ref[0:DH, lanes] * alpha + pv
@@ -308,11 +376,13 @@
     loads[10].wait()
     for n in range(6):
         cols = slice(n * 256, (n + 1) * 256)
-        base = hid_ref[:, cols] if n < 3 else x_ref[:, cols]
-        y = base.astype(F32) + nn_dot(att_ref[...], wo_ref[:, cols])
+        base = (hid_ref[:, cols] if n < 3 else x_ref[:, cols]).astype(F32)
+        if n < 3:
+            base = jnp.concatenate([he_ref[0:8, cols], base[8:-8], he_ref[8:16, cols]], axis=0)
+        y = base + nn_dot(att_ref[...], wo_ref[:, cols])
         out_ref[:, cols] = y.astype(BF)
 
-    for cp in halo + sends:
+    for cp in halo + sends + edges:
         cp.wait_send()
 
 
@@ -337,17 +407,23 @@
             pltpu.VMEM((ROWS, CO), BF),
             pltpu.VMEM((ROWS, C), BF),
             pltpu.VMEM((HEADS * ROWS, DH), BF),
-            pltpu.VMEM((32, ROWS, DH), BF),
+            pltpu.VMEM((32, BULK, DH), BF),
             pltpu.VMEM((32, DH, ROWS), BF),
             pltpu.VMEM((2, 256 * max(len(c) for c in CHUNKS), ROWS), F32),
             pltpu.VMEM((ROWS, HEADS * ROWS), F32),
             pltpu.VMEM((16, HEADS * ROWS), F32),
             pltpu.VMEM((ROWS, HEADS * DH), BF),
+            pltpu.VMEM((ROWS, HEADS * DH), F32),
+            pltpu.VMEM((16, CO), F32),
+            pltpu.VMEM((2, 4, 4, 16, 2 * DH), BF),
+            pltpu.VMEM((2, DH, 256), BF),
             pltpu.SemaphoreType.DMA((11,)),
             pltpu.SemaphoreType.DMA((2,)),
             pltpu.SemaphoreType.DMA((2,)),
             pltpu.SemaphoreType.DMA((62,)),
             pltpu.SemaphoreType.DMA((2, 32)),
+            pltpu.SemaphoreType.DMA((7,)),
+            pltpu.SemaphoreType.DMA((7,)),
         ],
         compiler_params=pltpu.CompilerParams(
             collective_id=0, has_side_effects=True, vmem_limit_bytes=40 << 20

time: 34.7 us -> 32.7 us (0.942)
  Pallas kernels: 33.8 us -> 31.7 us
    pallas_call x1, Pallas kernels: 33.8 us -> 31.7 us  [body(): pl.pallas_call(kernel, out_shape=jax.ShapeDtypeStruct((ROWS, C), BF), in_...]
where the time goes in v3:
time: 32.7 us; the launch traced here: 32.6 us
  Pallas kernels  31.7 us (97%)
  local copies, waits for them, and re-layouts  0.88 us (3%)
    pallas_call x1, Pallas kernels, body(): pl.pallas_call(kernel, out_shape=jax.ShapeDtypeStruct((ROWS, C), BF), in_...  31.7 us
    unnamed x1, local copies, waits for them, and re-layouts  0.88 us

profile of v3, /device:TPU:1, one launch (start us, length us, event | category | flops | bytes accessed | tf_op | source)
XLA Modules:
  0.0 32.6 jit_solution(4091730868021203486)
XLA Ops:
  0.0 31.7 %block.1 = bf16[256,1536]{1,0:T(8,128)(2,1)S(1)} custom-call(bf16[256,1536]{1,0:T(8,128)(2,1)} %x_hbm.1, f32[1536]{0:T(1024)} %cg_hbm.1, bf16[3,1536,768]{2,1,0:T(8,128)(2,1)} %cw_hbm.1, f32[768]{0:T(1024)} %cb_hbm.1, f32[1536]{0:T(1024)} %ag_hbm.1, bf16[1536,512]{1,0:T(8,128)(2,1)} %wq_hbm.1, bf16[1536,128]{1,0:T(8,128)(2,1)} %wk_hbm.1, ...), custom_call_target="tpu_custom_call" | custom-call | tf_op jit(solution)/shard_map/block/pallas_call | solution.py:391
  31.7 0.9 %copy.11 = bf16[256,1536]{1,0:T(8,128)(2,1)} copy(bf16[256,1536]{1,0:T(8,128)(2,1)S(1)} %block.1) | data formatting | bytes 1572864

commit v4 on v3

--- a/solution.py
+++ b/solution.py
@@ -19,7 +19,7 @@
 
 FAR = (2,)
 FAR_A = False
-LATE_B = False
+LATE_B = True
 EDGE_AT = (3, 7, 9)
 CHUNKS = (
     ((0, 0, 0), (1, 0, 0),),
@@ -37,16 +37,26 @@
 )
 ACTS = {
     (0, 0): ((1, 0, 0, 0), (1, 0, 0, 1),),
-    (0, 3): ((0, 1, 0, 0), (0, 3, 0, 0), (0, 0, 1, 0), (0, 0, 3, 0), (0, 3, 0, 1), (0, 1, 0, 1), (0, 0, 3, 1), (0, 0, 1, 1),),
-    (1, 3): ((1, 1, 0, 0), (1, 3, 0, 0), (1, 3, 0, 1), (1, 1, 0, 1),),
-    (2, 3): ((0, 2, 0, 0), (0, 1, 3, 0), (0, 1, 1, 0), (0, 3, 3, 0), (1, 0, 1, 0), (1, 0, 3, 0), (1, 0, 3, 1), (1, 0, 1, 1), (0, 3, 1, 0), (0, 2, 0, 1),),
-    (3, 3): ((0, 0, 2, 0), (0, 3, 3, 1), (1, 2, 0, 0), (1, 2, 0, 1), (0, 3, 1, 1), (0, 1, 3, 1),),
-    (4, 3): ((0, 1, 1, 1), (0, 0, 2, 1), (1, 3, 3, 0), (1, 3, 3, 1),),
-    (5, 3): ((0, 2, 1, 0), (0, 2, 3, 0), (1, 1, 3, 0), (1, 3, 1, 0), (1, 3, 1, 1), (1, 1, 3, 1),),
-    (6, 3): ((0, 2, 2, 0), (0, 1, 2, 0), (0, 2, 3, 1), (1, 1, 1, 0), (1, 0, 2, 0), (1, 1, 1, 1), (1, 0, 2, 1),),
-    (7, 3): ((0, 3, 2, 0), (1, 2, 3, 0), (0, 2, 1, 1), (0, 3, 2, 1), (1, 2, 3, 1),),
-    (8, 3): ((0, 1, 2, 1), (0, 2, 2, 1), (1, 2, 1, 0), (1, 2, 1, 1),),
-    (10, 3): ((1, 2, 2, 0), (1, 1, 2, 0), (1, 3, 2, 0), (1, 3, 2, 1), (1, 1, 2, 1), (1, 2, 2, 1),),
+    (0, 3): ((0, 1, 0, 0), (0, 3, 0, 0), (0, 0, 1, 0),),
+    (1, 0): ((0, 0, 3, 0), (0, 3, 0, 1), (0, 1, 0, 1), (0, 0, 3, 1), (0, 0, 1, 1),),
+    (1, 3): ((1, 1, 0, 0), (1, 3, 0, 0),),
+    (2, 0): ((0, 2, 0, 0), (0, 1, 3, 0), (1, 3, 0, 1), (1, 1, 0, 1),),
+    (2, 3): ((0, 1, 1, 0), (0, 3, 3, 0), (1, 0, 1, 0), (1, 0, 3, 0),),
+    (3, 0): ((1, 0, 3, 1), (1, 0, 1, 1), (0, 3, 1, 0), (0, 2, 0, 1),),
+    (3, 3): ((0, 0, 2, 0), (0, 3, 3, 1), (1, 2, 0, 0),),
+    (4, 0): ((1, 2, 0, 1), (0, 3, 1, 1), (0, 1, 3, 1),),
+    (4, 3): ((0, 1, 1, 1), (0, 0, 2, 1), (1, 3, 3, 0),),
+    (5, 0): ((1, 3, 3, 1),),
+    (5, 3): ((0, 2, 1, 0), (0, 2, 3, 0), (1, 1, 3, 0), (1, 3, 1, 0),),
+    (6, 0): ((0, 2, 2, 0), (1, 3, 1, 1), (1, 1, 3, 1),),
+    (6, 3): ((0, 1, 2, 0), (0, 2, 3, 1), (1, 1, 1, 0), (1, 0, 2, 0),),
+    (7, 0): ((0, 3, 2, 0), (1, 1, 1, 1), (1, 0, 2, 1),),
+    (7, 3): ((0, 2, 1, 1), (0, 3, 2, 1), (1, 2, 3, 0),),
+    (8, 0): ((1, 2, 3, 1),),
+    (8, 3): ((0, 1, 2, 1), (0, 2, 2, 1), (1, 2, 1, 0),),
+    (9, 0): ((1, 2, 1, 1),),
+    (10, 3): ((1, 2, 2, 0), (1, 1, 2, 0), (1, 3, 2, 0),),
+    (11, 0): ((1, 3, 2, 1), (1, 1, 2, 1), (1, 2, 2, 1),),
 }
 
 

time: 32.7 us -> 33 us (level)
  no operation moved by 1% of the time
where the time goes in v4:
time: 33 us; the launch traced here: 32.9 us
  Pallas kernels  32 us (97%)
  local copies, waits for them, and re-layouts  0.88 us (3%)
    pallas_call x1, Pallas kernels, body(): pl.pallas_call(kernel, out_shape=jax.ShapeDtypeStruct((ROWS, C), BF), in_...  32 us
    unnamed x1, local copies, waits for them, and re-layouts  0.88 us

profile of v4, /device:TPU:1, one launch (start us, length us, event | category | flops | bytes accessed | tf_op | source)
XLA Modules:
  0.0 32.9 jit_solution(14632177176426482015)
XLA Ops:
  0.0 32.0 %block.1 = bf16[256,1536]{1,0:T(8,128)(2,1)S(1)} custom-call(bf16[256,1536]{1,0:T(8,128)(2,1)} %x_hbm.1, f32[1536]{0:T(1024)} %cg_hbm.1, bf16[3,1536,768]{2,1,0:T(8,128)(2,1)} %cw_hbm.1, f32[768]{0:T(1024)} %cb_hbm.1, f32[1536]{0:T(1024)} %ag_hbm.1, bf16[1536,512]{1,0:T(8,128)(2,1)} %wq_hbm.1, bf16[1536,128]{1,0:T(8,128)(2,1)} %wk_hbm.1, ...), custom_call_target="tpu_custom_call" | custom-call | tf_op jit(solution)/shard_map/block/pallas_call | solution.py:401
  32.0 0.9 %copy.11 = bf16[256,1536]{1,0:T(8,128)(2,1)} copy(bf16[256,1536]{1,0:T(8,128)(2,1)S(1)} %block.1) | data formatting | bytes 1572864
